TPU v7x, 256 devices: a whole 4x4x8 slice. The times are simulated.
256 devices in a mesh: row: 16 (over y, x), col: 8 (over z_lo, core), band: 2 (over z_hi).
Axes of the slice: x: 4, y: 4, z: 8 (z_hi: 2, z_lo: 4; z = z_hi * 4 + z_lo), core: 2. Of those that a mesh axis runs over, the one named last changes fastest.
Arguments:
- panel: bfloat16 [32, 512, 512], P('row', ('col', 'band')), may hold values from -6 to 6
- inverse: bfloat16 [2, 512, 512], replicated, may hold values from -0.25 to 0.25
- trail_grad: bfloat16 [32, 32, 512, 512], P('row', ('col', 'band')), may hold values from -0.046875 to 0.046875
- factor_grad: bfloat16 [32, 512, 512], P('row', ('col', 'band')), may hold values from -6 to 6
- present: int32 [32, 32], P('row', ('col', 'band')), may hold values from 0 to 1, as said below
- supernode: int32 [32], replicated, may hold values from 0 to 1
Outputs:
- panel_adjoint: bfloat16 [32, 512, 512], P('row', ('col', 'band'))
- inverse_adjoint: float32 [2, 512, 512], replicated
Inputs may be any that keep to these rules, and one draw needn't show every extreme that they name: Every diagonal tile is present; rows differ widely in how many tiles are present.
All inputs are finite; a program needn't handle non-finite values.
Results may differ from a plain program's by a relative error of at most 0.0055.
Values may be sent and summed in bfloat16 or wider, within the bound.
A program may use at most 64 MiB of HBM per device.

v0:
```python
import jax
import jax.numpy as jnp
from jax import lax
from jax.sharding import PartitionSpec as P


def from_root(value, axis, source):
    kept = jnp.where(lax.axis_index(axis) == source, value, 0).astype(value.dtype)
    return lax.psum(kept, axis)


def pick_inverse(inverse, labels):
    first = inverse[0][None, :, :]
    second = inverse[1][None, :, :]
    return jnp.where((labels == 0)[:, None, None], first, second)


def local(panel, inverse, trail_grad, factor_grad, present, supernode):
    rows_here = trail_grad.shape[0]
    cols_here = trail_grad.shape[1]
    tile = trail_grad.shape[2]
    total_rows = rows_here * lax.axis_size("row")
    row_index = lax.axis_index("row")
    col_index = lax.axis_index(("col", "band"))
    row_labels = lax.dynamic_slice_in_dim(supernode, row_index * rows_here, rows_here)
    col_labels = lax.dynamic_slice_in_dim(supernode, col_index * cols_here, cols_here)
    root = col_index * cols_here // rows_here
    row_inverse = pick_inverse(inverse, row_labels)
    factor_piece = jnp.einsum(
        "iab,ibc->iac", panel, row_inverse, preferred_element_type=jnp.float32
    ).astype(jnp.bfloat16)
    factor_row = lax.all_gather(factor_piece, ("col", "band"), axis=1, tiled=True)
    factor_block = from_root(factor_row, "row", root)
    weight = present * (row_labels[:, None] == col_labels[None, :]).astype(jnp.int32)
    masked = trail_grad * weight.astype(jnp.bfloat16)[:, :, None, None]
    mirror_part = jnp.einsum(
        "ijab,iae->jbe", masked, factor_row, preferred_element_type=jnp.float32
    )
    mirror = lax.psum(mirror_part, "row")
    mirror_cols = jnp.transpose(mirror, (1, 0, 2))
    is_owner = (row_index == root).astype(jnp.float32)
    placed = mirror_cols
    placed = placed * is_owner
    direct = jnp.einsum("ijab,jbe->aie", masked, factor_block, preferred_element_type=jnp.float32)
    summed = lax.psum_scatter(direct + placed, ("col", "band"), scatter_dimension=0, tiled=True)
    factor_total = (jnp.transpose(factor_grad.astype(jnp.float32), (1, 0, 2)) - summed).astype(
        jnp.bfloat16
    )
    panel_adjoint = jnp.einsum(
        "aie,ife->iaf", factor_total, row_inverse, preferred_element_type=jnp.float32
    ).astype(jnp.bfloat16)
    onehot = (row_labels[:, None] == jnp.arange(2, dtype=jnp.int32)[None, :]).astype(jnp.float32)
    terms = jnp.einsum("iaf,aie->ife", panel, factor_total, preferred_element_type=jnp.float32)
    local_grad = jnp.einsum("is,ife->sfe", onehot, terms)
    inverse_adjoint = lax.psum(local_grad, ("row", "col", "band")) / jnp.sqrt(
        jnp.float32(total_rows * tile)
    )
    return (panel_adjoint, inverse_adjoint)


def solution(mesh):
    in_specs = (
        P("row", ("col", "band"), None),
        P(),
        P("row", ("col", "band"), None, None),
        P("row", ("col", "band"), None),
        P("row", ("col", "band")),
        P(),
    )
    out_specs = (P("row", ("col", "band"), None), P())
    return jax.shard_map(local, mesh=mesh, in_specs=in_specs, out_specs=out_specs, check_vma=False)
```

profile of v0, /device:TPU:2, one launch (start us, length us, event | category | flops | bytes accessed | tf_op | source)
XLA Modules:
  0.0 711.1 jit_solution(867655354191725240)
XLA Ops:
  7.2 0.0 all-gather.2.cloned.1.call-start
  7.2 1.3 slice_bitcast_fusion.1
  8.5 0.1 broadcast_compare_fusion
  8.6 1.1 fusion.19
  9.7 0.0 all-gather.2.cloned.1.call-update
  9.7 0.0 all-reduce.6.cloned.1.call-start
  9.8 92.1 %all-gather.2.cloned.1.call-done = bf16[2,512,512]{2,1,0:T(8,128)(2,1)} async-done(((bf16[2,32,512]{2,1,0:T(8,128)(2,1)}), bf16[2,512,512]{2,1,0:T(8,128)(2,1)}) %all-gather.2.cloned.1.call-update) | async-done | bytes 1048592 | tf_op jit(solution)/shard_map/all_gather | solution.py:32
  101.9 1.1 broadcast_select_fusion
  103.0 0.0 all-reduce.8.cloned.1.call-start
  103.1 0.1 dynamic_slice.7
  103.2 0.1 fusion.36
  103.2 0.3 copy-done.1
  103.5 4.2 fusion.4
  107.8 0.0 all-reduce.8.cloned.1.call-update
  107.8 0.0 all-reduce.12.cloned.1.call-start
  107.8 96.2 %all-reduce.6.cloned.1.call-done = bf16[2,512,512]{2,1,0:T(8,128)(2,1)} async-done(((bf16[2,512,512]{2,1,0:T(8,128)(2,1)}), bf16[2,512,512]{2,1,0:T(8,128)(2,1)}) %all-reduce.6.cloned.1.call-update) | async-done | bytes 1048592 | tf_op jit(solution)/shard_map/psum | solution.py:9
  204.0 104.7 %all-reduce.8.cloned.1.call-done = f32[2,512,512]{1,2,0:T(8,128)} async-done(((f32[2,512,512]{1,2,0:T(8,128)}), f32[2,512,512]{1,2,0:T(8,128)}) %all-reduce.8.cloned.1.call-update) | async-done | bytes 2097168 | tf_op jit(solution)/shard_map/psum | solution.py:39
  308.8 3.9 bitcast_add_fusion
  312.7 2.4 copy.26
  315.1 0.0 all-reduce.12.cloned.1.call-update
  315.1 0.0 all-reduce.10.cloned.1.call-start
  315.2 0.6 copy-done.5
  315.8 0.6 dynamic-slice
  317.0 113.6 %all-reduce.12.cloned.1.call-done = f32[512,2,512]{2,1,0:T(2,128)} async-done(((f32[512,2,512]{2,1,0:T(2,128)}), f32[512,2,512]{2,1,0:T(2,128)}) %all-reduce.12.cloned.1.call-update) | async-done | bytes 2097168
  430.6 0.9 constant_dynamic-slice_fusion
  431.6 0.5 convolution_bitcast_fusion
  432.1 1.0 copy.29
  433.1 2.8 fusion.33
  435.9 1.1 fusion.16
  437.0 263.4 %all-reduce.10.cloned.1.call-done = f32[2,512,512]{2,0,1:T(2,128)} async-done(((f32[2,512,512]{2,0,1:T(2,128)}), f32[2,512,512]{2,0,1:T(2,128)}) %all-reduce.10.cloned.1.call-update) | async-done | bytes 2097168 | tf_op jit(solution)/shard_map/psum | solution.py:55
  700.4 2.5 broadcast_multiply_fusion
  702.9 1.7 copy.30
  (12 shorter events, 0.1 us)
Async XLA Ops:
  7.2 1.4 copy-start
  7.2 1.3 copy-start.4
  7.2 94.7 %all-gather.2.cloned.1.call-start = ((), (), s32[]{:S(2)}) async-start(), calls=%async_computation | async-start | bytes 1114112 | tf_op jit(solution)/shard_map/all_gather | solution.py:32
  8.6 94.6 %copy-start.3 = (s32[2,2]{1,0:T(2,128)S(1)}, s32[2,2]{1,0:T(2,128)}, u32[]{:S(2)}) copy-start(s32[2,2]{1,0:T(2,128)} %param.10) | copy-start | bytes 52
  9.7 194.3 %all-reduce.6.cloned.1.call-start = ((), (), s32[]{:S(2)}) async-start(), calls=%async_computation.1 | async-start | bytes 2097152 | tf_op jit(solution)/shard_map/psum | solution.py:9
  101.9 1.6 copy-start.1
  103.0 205.7 %all-reduce.8.cloned.1.call-start = ((), (), s32[]{:S(2)}) async-start(), calls=%async_computation.2 | async-start | bytes 4194304 | tf_op jit(solution)/shard_map/psum | solution.py:39
  107.8 322.9 %all-reduce.12.cloned.1.call-start = ((), (), s32[]{:S(2)}) async-start(), calls=%async_computation.4 | async-start | bytes 4194304
  315.1 0.7 copy-start.5
  315.1 116.5 %copy-start.2 = (bf16[2,32,512]{2,1,0:T(8,128)(2,1)S(1)}, bf16[2,32,512]{2,1,0:T(8,128)(2,1)}, u32[]{:S(2)}) copy-start(bf16[2,32,512]{2,1,0:T(8,128)(2,1)} %param.9) | copy-start | bytes 196612
  315.1 385.3 %all-reduce.10.cloned.1.call-start = ((), (), s32[]{:S(2)}) async-start(), calls=%async_computation.3 | async-start | bytes 4194304 | tf_op jit(solution)/shard_map/psum | solution.py:55
Sparse Core Ops, SparseCore 0:
  10.4 91.5 all-gather.1
  105.2 98.8 all-reduce.5
  207.9 100.7 all-reduce.7
  315.3 115.3 all-reduce.11
  436.4 263.9 all-reduce.9
where the time goes:
time: 711 us
  waiting for transfers between devices  670 us (94%)
  between operations  14.5 us (2%)
  matrix products  13.7 us (2%)
  local copies, waits for them, and re-layouts  8.87 us (1%)
    psum x1, waiting for transfers between devices, local(): lax.psum(local_grad, ('row', 'col', 'band'))  263 us
    unnamed x6, waiting for transfers between devices  114 us
    psum x1, waiting for transfers between devices, local(): mirror = lax.psum(mirror_part, 'row')  105 us
    psum x1, waiting for transfers between devices, from_root(): return lax.psum(kept, axis)  96.2 us
    all_gather x1, waiting for transfers between devices, local(): lax.all_gather(factor_piece, ('col', 'band'), axis=1, tiled=True)  92.1 us
  transfers between devices with their start and end apart: 5, of which 5 were waited for; matrix products, arithmetic and copies ran while one was open for 1% of the time, Pallas kernels for 0%

commit v1 on v0

--- a/solution.py
+++ b/solution.py
@@ -36,7 +36,11 @@
     mirror_part = jnp.einsum(
         "ijab,iae->jbe", masked, factor_row, preferred_element_type=jnp.float32
     )
-    mirror = lax.psum(mirror_part, "row")
+    count = lax.axis_size("row")
+    mirror, reach = (mirror_part, 1)
+    while reach < count:
+        mirror = mirror + lax.ppermute(mirror, "row", [(i, i ^ reach) for i in range(count)])
+        reach = 2 * reach
     mirror_cols = jnp.transpose(mirror, (1, 0, 2))
     is_owner = (row_index == root).astype(jnp.float32)
     placed = mirror_cols

time: 711 us -> 783 us (1.10)
  waiting for transfers between devices: 670 us -> 730 us
    ppermute x0 -> x4, waiting for transfers between devices: none -> 141 us  [local(): lax.ppermute(mirror, 'row', [(i, i ^ reach) for i in range(count)])]
    psum x1 -> x0, waiting for transfers between devices: 105 us -> none  [local(): mirror = lax.psum(mirror_part, 'row')]
    psum x1, waiting for transfers between devices: 96.2 us -> 120 us  [from_root(): return lax.psum(kept, axis)]
    unnamed x6 -> x5, waiting for transfers between devices: 114 us -> 114 us
  transfers between devices with their start and end apart: 5 -> 8, of which waited for: 5 -> 7; matrix products, arithmetic and copies ran while one was open for 1% -> 1% of each run, Pallas kernels for 0% -> 0%
where the time goes in v1:
time: 783 us
  waiting for transfers between devices  730 us (93%)
  between operations  14.6 us (2%)
  matrix products  12 us (2%)
  local copies, waits for them, and re-layouts  10.3 us (1%)
  other arithmetic  8.79 us (1%)
    psum x1, waiting for transfers between devices, local(): lax.psum(local_grad, ('row', 'col', 'band'))  263 us
    ppermute x4, waiting for transfers between devices, local(): lax.ppermute(mirror, 'row', [(i, i ^ reach) for i in range(count)])  141 us
    psum x1, waiting for transfers between devices, from_root(): return lax.psum(kept, axis)  120 us
    unnamed x5, waiting for transfers between devices  114 us
    all_gather x1, waiting for transfers between devices, local(): lax.all_gather(factor_piece, ('col', 'band'), axis=1, tiled=True)  92 us
  transfers between devices with their start and end apart: 8, of which 7 were waited for; matrix products, arithmetic and copies ran while one was open for 1% of the time, Pallas kernels for 0%

profile of v1, /device:TPU:2, one launch (start us, length us, event | category | flops | bytes accessed | tf_op | source)
XLA Modules:
  0.0 782.8 jit_solution(18381853403996225362)
XLA Ops:
  7.3 1.3 slice_bitcast_fusion.1
  8.6 0.1 broadcast_compare_fusion
  8.6 1.1 fusion.17
  9.8 0.1 dynamic_slice.7
  10.0 92.0 %all-gather.2.cloned.1.call-done = bf16[2,512,512]{2,1,0:T(8,128)(2,1)} async-done(((bf16[2,32,512]{2,1,0:T(8,128)(2,1)}), bf16[2,512,512]{2,1,0:T(8,128)(2,1)}) %all-gather.2.cloned.1.call-update) | async-done | bytes 1048592 | tf_op jit(solution)/shard_map/all_gather | solution.py:32
  101.9 3.2 fusion.4
  105.1 0.1 collective-permute-start
  105.2 48.4 %collective-permute-done = f32[2,512,512]{1,2,0:T(8,128)S(1)} collective-permute-done((f32[2,512,512]{1,2,0:T(8,128)S(1)}, f32[2,512,512]{1,2,0:T(8,128)S(1)}, u32[]{:S(2)}, u32[]{:S(2)}) %collective-permute-start) | collective-permute-done | bytes 2097184 | tf_op jit(solution)/shard_map/ppermute | solution.py:42
  153.6 0.5 add.34
  154.1 2.2 collective-permute-start.1
  156.3 47.0 %collective-permute-done.1 = f32[2,512,512]{1,2,0:T(8,128)S(1)} collective-permute-done((f32[2,512,512]{1,2,0:T(8,128)S(1)}, f32[2,512,512]{1,2,0:T(8,128)S(1)}, u32[]{:S(2)}, u32[]{:S(2)}) %collective-permute-start.1) | collective-permute-done | bytes 2097184 | tf_op jit(solution)/shard_map/ppermute | solution.py:42
  203.3 0.5 add.35
  203.8 1.7 collective-permute-start.2
  205.6 45.1 %collective-permute-done.2 = f32[2,512,512]{1,2,0:T(8,128)S(1)} collective-permute-done((f32[2,512,512]{1,2,0:T(8,128)S(1)}, f32[2,512,512]{1,2,0:T(8,128)S(1)}, u32[]{:S(2)}, u32[]{:S(2)}) %collective-permute-start.2) | collective-permute-done | bytes 2097184 | tf_op jit(solution)/shard_map/ppermute | solution.py:42
  250.7 0.5 add.36
  251.2 3.3 collective-permute-start.3
  254.5 1.0 broadcast_select_fusion
  255.6 119.9 %all-reduce.5.cloned.1.call-done = bf16[2,512,512]{2,1,0:T(8,128)(2,1)} async-done(((bf16[2,512,512]{2,1,0:T(8,128)(2,1)}), bf16[2,512,512]{2,1,0:T(8,128)(2,1)}) %all-reduce.5.cloned.1.call-update) | async-done | bytes 1048592 | tf_op jit(solution)/shard_map/psum | solution.py:9
  375.5 3.3 fusion.2
  378.8 3.7 bitcast_add_fusion
  382.5 4.1 copy.29
  386.7 0.6 copy-done.9
  387.3 0.6 dynamic-slice
  388.5 113.8 %all-reduce.9.cloned.1.call-done = f32[512,2,512]{2,1,0:T(2,128)} async-done(((f32[512,2,512]{2,1,0:T(2,128)}), f32[512,2,512]{2,1,0:T(2,128)}) %all-reduce.9.cloned.1.call-update) | async-done | bytes 2097168
  502.3 0.9 constant_dynamic-slice_fusion
  503.2 0.5 convolution_bitcast_fusion
  503.7 1.0 copy.32
  504.7 2.8 fusion.31
  507.6 1.1 fusion.14
  508.7 263.4 %all-reduce.7.cloned.1.call-done = f32[2,512,512]{2,0,1:T(2,128)} async-done(((f32[2,512,512]{2,0,1:T(2,128)}), f32[2,512,512]{2,0,1:T(2,128)}) %all-reduce.7.cloned.1.call-update) | async-done | bytes 2097168 | tf_op jit(solution)/shard_map/psum | solution.py:59
  772.1 2.5 broadcast_multiply_fusion
  774.6 1.7 copy.33
  (29 shorter events, 0.3 us)
Async XLA Ops:
  7.2 1.5 copy-start
  7.2 1.4 copy-start.8
  7.2 2.7 copy-start.7
  7.2 94.7 %all-gather.2.cloned.1.call-start = ((), (), s32[]{:S(2)}) async-start(), calls=%async_computation | async-start | bytes 1114112 | tf_op jit(solution)/shard_map/all_gather | solution.py:32
  8.5 96.6 %copy-start.2 = (bf16[512,512]{1,0:T(8,128)(2,1)}, bf16[512,512]{1,0:T(8,128)(2,1)S(1)}, u32[]{:S(2)}) copy-start(bf16[512,512]{1,0:T(8,128)(2,1)S(1)} %get-tuple-element.10) | copy-start | bytes 1572868
  8.5 96.6 %copy-start.4 = (bf16[512,512]{1,0:T(8,128)(2,1)}, bf16[512,512]{1,0:T(8,128)(2,1)S(1)}, u32[]{:S(2)}) copy-start(bf16[512,512]{1,0:T(8,128)(2,1)S(1)} %get-tuple-element.11) | copy-start | bytes 1572868
  9.7 365.8 %all-reduce.5.cloned.1.call-start = ((), (), s32[]{:S(2)}) async-start(), calls=%async_computation.1 | async-start | bytes 2097152 | tf_op jit(solution)/shard_map/psum | solution.py:9
  105.1 48.5 %collective-permute-start = (f32[2,512,512]{1,2,0:T(8,128)S(1)}, f32[2,512,512]{1,2,0:T(8,128)S(1)}, u32[]{:S(2)}, u32[]{:S(2)}) collective-permute-start(f32[2,512,512]{1,2,0:T(8,128)S(1)} %fusion.4), channel_id=1, source_target_pairs={{0,16},{16,0},{32,48},{48,32},{64,80},{80,64},{96,112},{112,96},{1... | collective-permute-start | bytes 6291464 | tf_op jit(solution)/shard_map/ppermute | solution.py:42
  154.1 49.2 %collective-permute-start.1 = (f32[2,512,512]{1,2,0:T(8,128)S(1)}, f32[2,512,512]{1,2,0:T(8,128)S(1)}, u32[]{:S(2)}, u32[]{:S(2)}) collective-permute-start(f32[2,512,512]{1,2,0:T(8,128)S(1)} %add.34), channel_id=1, source_target_pairs={{0,32},{16,48},{32,0},{48,16},{64,96},{80,112},{96,64},{112,80},{1... | collective-permute-start | bytes 6291464 | tf_op jit(solution)/shard_map/ppermute | solution.py:42
  203.8 50.6 %copy-start.1 = (bf16[2,512,512]{2,1,0:T(8,128)(2,1)S(1)}, bf16[2,512,512]{2,1,0:T(8,128)(2,1)}, u32[]{:S(2)}) copy-start(bf16[2,512,512]{2,1,0:T(8,128)(2,1)} %all-gather.2.cloned.1.call-done) | copy-start | bytes 3145732
  203.8 46.9 %collective-permute-start.2 = (f32[2,512,512]{1,2,0:T(8,128)S(1)}, f32[2,512,512]{1,2,0:T(8,128)S(1)}, u32[]{:S(2)}, u32[]{:S(2)}) collective-permute-start(f32[2,512,512]{1,2,0:T(8,128)S(1)} %add.35), channel_id=1, source_target_pairs={{0,64},{16,80},{32,96},{48,112},{64,0},{80,16},{96,32},{112,48},{1... | collective-permute-start | bytes 6291464 | tf_op jit(solution)/shard_map/ppermute | solution.py:42
  251.2 127.6 %collective-permute-start.3 = (f32[2,512,512]{1,2,0:T(8,128)S(1)}, f32[2,512,512]{1,2,0:T(8,128)}, u32[]{:S(2)}, u32[]{:S(2)}) collective-permute-start(f32[2,512,512]{1,2,0:T(8,128)S(1)} %add.36), channel_id=1, source_target_pairs={{0,128},{16,144},{32,160},{48,176},{64,192},{80,208},{96,224},{112... | collective-permute-start | bytes 6291464 | tf_op jit(solution)/shard_map/ppermute | solution.py:42
  255.5 246.8 %all-reduce.9.cloned.1.call-start = ((), (), s32[]{:S(2)}) async-start(), calls=%async_computation.3 | async-start | bytes 4194304
  386.6 0.7 copy-start.9
  386.6 116.6 %copy-start.6 = (bf16[2,32,512]{2,1,0:T(8,128)(2,1)S(1)}, bf16[2,32,512]{2,1,0:T(8,128)(2,1)}, u32[]{:S(2)}) copy-start(bf16[2,32,512]{2,1,0:T(8,128)(2,1)} %param.9) | copy-start | bytes 196612
  386.6 385.5 %all-reduce.7.cloned.1.call-start = ((), (), s32[]{:S(2)}) async-start(), calls=%async_computation.2 | async-start | bytes 4194304 | tf_op jit(solution)/shard_map/psum | solution.py:59
  504.7 2.9 copy-start.3
  504.7 2.9 copy-start.5
Sparse Core Ops, SparseCore 0:
  10.4 91.5 all-gather.1
  255.6 119.8 all-reduce.4
  386.8 115.5 all-reduce.8
  508.1 263.9 all-reduce.6
